TPU v7x, 32 devices: a whole 2x2x4 slice. The times are simulated.
32 devices in a mesh: ctx: 8 (over y, x, core), tp: 4 (over z).
Axes of the slice: x: 2, y: 2, z: 4, core: 2. Of those that a mesh axis runs over, the one named last changes fastest.
Arguments:
- query_mr: bfloat16 [2048, 8192], P('ctx', 'tp'), may hold values from -6 to 6
- key_mr: bfloat16 [2048, 8192], P('ctx', 'tp'), may hold values from -6 to 6
- value_mr: bfloat16 [2048, 8192], P('ctx', 'tp'), may hold values from -6 to 6
- query_li: bfloat16 [2048, 8192], P('ctx', 'tp'), may hold values from -6 to 6
- key_li: bfloat16 [2048, 8192], P('ctx', 'tp'), may hold values from -6 to 6
- cotangent: bfloat16 [2048, 8192], P('ctx', 'tp'), may hold values from -6 to 6
- mr_taps: float32 [128, 8192], P(None, 'tp'), may hold values from -0.5 to 0.5
- decay_rates: float32 [8], replicated, may hold values from 4.8828126e-05 to 0.03
- residues: float32 [8, 8192], P(None, 'tp'), may hold values from -2 to 2
Outputs:
- grad_query_mr: bfloat16 [2048, 8192], P('ctx', 'tp')
- grad_key_mr: bfloat16 [2048, 8192], P('ctx', 'tp')
- grad_value_mr: bfloat16 [2048, 8192], P('ctx', 'tp')
- grad_query_li: bfloat16 [2048, 8192], P('ctx', 'tp')
- grad_key_li: bfloat16 [2048, 8192], P('ctx', 'tp')
- grad_taps: float32 [128, 8192], P(None, 'tp')
- grad_residues: float32 [8, 8192], P(None, 'tp')
All inputs are finite; a program needn't handle non-finite values.
Results may differ from a plain program's by a relative error of at most 0.001.
Values may be sent and summed in bfloat16 or wider, within the bound.
A program may use at most 128 MiB of HBM per device.

v0:
```python
import math
import jax
import jax.numpy as jnp
from jax import lax
from jax.sharding import PartitionSpec as P

BLOCK = 128
highest = lax.Precision.HIGHEST


def from_behind(value, axis, by):
    size = lax.axis_size(axis)
    pairs = [(i, i + by) for i in range(size) if 0 <= i + by < size]
    return lax.ppermute(value, axis, pairs)


def depthwise(signal, kernel):
    channels = signal.shape[1]
    output = lax.conv_general_dilated(
        signal[None],
        kernel[:, None, :],
        (1,),
        "VALID",
        dimension_numbers=("NWC", "WIO", "NWC"),
        feature_group_count=channels,
        precision=highest,
    )
    return output[0]


def linked(earlier, later):
    return (earlier[0] * later[1] + later[0], earlier[1] * later[1])


def modal_terms(inputs, cotangents, decay_rates, residues, block_len):
    length, channels = inputs.shape
    blocks = length // block_len
    in_blocks = inputs.reshape(blocks, block_len, channels)
    co_blocks = cotangents.reshape(blocks, block_len, channels)
    places = jnp.arange(block_len, dtype=jnp.float32)
    offsets = places[:, None] - places[None, :]
    modes = decay_rates.shape[0]

    def one_mode(mode, state):
        conv_sum, back_sum, residue_grad, end_rows, start_rows = state
        decay_rate = decay_rates[mode]
        residue_row = lax.dynamic_index_in_dim(residues, mode, 0, keepdims=False)
        mode_scale = jnp.sqrt(-jnp.expm1(-2.0 * decay_rate))
        toeplitz = jnp.where(
            offsets >= 0.0, mode_scale * jnp.exp(-decay_rate * jnp.maximum(offsets, 0.0)), 0.0
        )
        block_pows = jnp.full((blocks, 1), jnp.exp(-decay_rate * block_len), jnp.float32)
        forward = jnp.einsum("tj,bjc->btc", toeplitz, in_blocks, precision=highest)
        backward = jnp.einsum("jt,bjc->btc", toeplitz, co_blocks, precision=highest)
        forward_incl = lax.associative_scan(linked, (forward[:, -1], block_pows))[0]
        backward_incl = lax.associative_scan(linked, (backward[:, 0], block_pows), reverse=True)[0]
        zero_row = jnp.zeros((1, channels), jnp.float32)
        forward_in = jnp.concatenate([zero_row, forward_incl[:-1]], 0)
        backward_in = jnp.concatenate([backward_incl[1:], zero_row], 0)
        lead_pows = jnp.exp(-decay_rate * (places + 1.0))
        tail_pows = jnp.exp(-decay_rate * (block_len - places))
        states = (forward + lead_pows[None, :, None] * forward_in[:, None, :]).reshape(
            length, channels
        )
        reverse_states = (backward + tail_pows[None, :, None] * backward_in[:, None, :]).reshape(
            length, channels
        )
        conv_sum = conv_sum + residue_row[None, :] * states
        back_sum = back_sum + residue_row[None, :] * reverse_states
        residue_grad = lax.dynamic_update_index_in_dim(
            residue_grad, jnp.sum(inputs * reverse_states, 0), mode, 0
        )
        end_rows = lax.dynamic_update_index_in_dim(end_rows, states[length - 1], mode, 0)
        start_rows = lax.dynamic_update_index_in_dim(start_rows, reverse_states[0], mode, 0)
        return (conv_sum, back_sum, residue_grad, end_rows, start_rows)

    zero_field = jnp.zeros((length, channels), jnp.float32)
    zero_modes = jnp.zeros((modes, channels), jnp.float32)
    return lax.fori_loop(
        0, modes, one_mode, (zero_field, zero_field, zero_modes, zero_modes, zero_modes)
    )


def per_device(
    query_mr, key_mr, value_mr, query_li, key_li, cotangent, mr_taps, decay_rates, residues
):
    length, channels = query_mr.shape
    taps_len = mr_taps.shape[0]
    rim_rows = taps_len - 1
    devices_ctx = lax.axis_size("ctx")
    seq_len = length * devices_ctx
    prior_key, prior_value = from_behind(
        (key_mr[length - rim_rows :], value_mr[length - rim_rows :]), "ctx", 1
    )
    key_first = key_mr.astype(jnp.float32)
    value_first = value_mr.astype(jnp.float32)
    query_first = query_mr.astype(jnp.float32)
    mixed_in = jnp.concatenate([prior_key, key_mr], 0).astype(jnp.float32) * jnp.concatenate(
        [prior_value, value_mr], 0
    ).astype(jnp.float32)
    mr_conv = depthwise(mixed_in, mr_taps[::-1])
    mr_out = query_first * mr_conv
    key_second = key_li.astype(jnp.float32)
    cotan = cotangent.astype(jnp.float32)
    li_input = key_second * mr_out
    li_cotan = cotan * query_li.astype(jnp.float32)
    regrouped = lax.all_to_all(
        jnp.stack([li_input, li_cotan]), "ctx", split_axis=2, concat_axis=1, tiled=True
    )
    piece_cols = channels // devices_ctx
    local_residues = lax.dynamic_slice_in_dim(
        residues, lax.axis_index("ctx") * piece_cols, piece_cols, 1
    )
    conv_seq, back_seq, residue_piece, unused_ends, unused_starts = modal_terms(
        regrouped[0], regrouped[1], decay_rates, local_residues, BLOCK
    )
    returned = lax.all_to_all(
        jnp.stack([conv_seq, back_seq]), "ctx", split_axis=1, concat_axis=2, tiled=True
    )
    li_conv = returned[0]
    li_back = returned[1]
    residue_sum = lax.all_gather(residue_piece, "ctx", axis=1, tiled=True)
    grad_query_li = (cotan * li_conv).astype(jnp.bfloat16)
    grad_key_li = (mr_out * li_back).astype(jnp.bfloat16)
    mr_grad = cotan + key_second * li_back
    grad_query_mr = (mr_grad * mr_conv).astype(jnp.bfloat16)
    mr_cotan = mr_grad * query_first
    next_rows = from_behind(mr_cotan[:rim_rows], "ctx", -1)
    mixed_grad = depthwise(jnp.concatenate([mr_cotan, next_rows], 0), mr_taps)
    grad_key_mr = (mixed_grad * value_first).astype(jnp.bfloat16)
    grad_value_mr = (mixed_grad * key_first).astype(jnp.bfloat16)
    tap_part = depthwise(mixed_in, mr_cotan)[::-1]
    tap_sum = lax.psum(tap_part, "ctx")
    factor = 1.0 / math.sqrt(seq_len)
    return (
        grad_query_mr,
        grad_key_mr,
        grad_value_mr,
        grad_query_li,
        grad_key_li,
        tap_sum * factor,
        residue_sum * factor,
    )


def solution(mesh):
    placed = (
        P("ctx", "tp"),
        P("ctx", "tp"),
        P("ctx", "tp"),
        P("ctx", "tp"),
        P("ctx", "tp"),
        P("ctx", "tp"),
        P(None, "tp"),
        P(),
        P(None, "tp"),
    )
    return jax.shard_map(
        per_device,
        mesh=mesh,
        in_specs=placed,
        out_specs=(
            P("ctx", "tp"),
            P("ctx", "tp"),
            P("ctx", "tp"),
            P("ctx", "tp"),
            P("ctx", "tp"),
            P(None, "tp"),
            P(None, "tp"),
        ),
        check_vma=False,
    )
```

profile of v0, /device:TPU:0, one launch (start us, length us, event | category | flops | bytes accessed | tf_op | source)
XLA Modules:
  0.0 570.9 jit_solution(17721856543120809470)
XLA Ops:
  9.3 2.4 collective-permute-start
  13.7 5.3 collective-permute-start.1
  19.0 8.9 %rev.15 = f32[128,2048]{1,0:T(8,128)} reverse(f32[128,2048]{1,0:T(8,128)} %param.17), dimensions={0} | reverse | bytes 2097152 | tf_op jit(solution)/shard_map/rev | solution.py:101
  31.3 21.5 %fusion.49 = f32[1,256,2048]{2,0,1:T(1,128)S(1)} fusion(f32[1,383,2048]{2,1,0:T(8,128)S(1)} %convert_multiply_fusion, f32[128,1,2048]{2,0,1:T(8,128)S(1)} %bitcast.140), kind=kOutput, calls=%fused_computation.100 | convolution fusion | flops 805306368 | bytes 6283264 | tf_op jit(solution)/shard_map/conv_general_dilated | solution.py:19
  54.4 2.5 pad_maximum_fusion.6
  56.9 7.3 %copy.48 = f32[2,256,2048]{1,0,2:T(2,128)} copy(f32[2,256,2048]{2,1,0:T(8,128)} %pad_maximum_fusion.6) | data formatting | bytes 8388608 | tf_op jit(solution)/shard_map/stack | solution.py:108
  64.1 4.6 all-to-all-start
  68.8 49.0 %all-to-all-done = f32[2,256,2048]{1,0,2:T(2,128)} async-done(((f32[2,256,2048]{1,0,2:T(2,128)}), f32[2,256,2048]{1,0,2:T(2,128)}, u32[]{:S(2)}, u32[]{:S(2)}) %all-to-all-start) | async-done | bytes 4194336 | tf_op jit(solution)/shard_map/all_to_all | solution.py:107
  117.8 9.6 %fusion.58 = (f32[1,8,256,256]{2,0,3,1:T(1,128)}, f32[1,8,256,256]{2,0,3,1:T(1,128)}) fusion(f32[2,8,256,256]{2,0,3,1:T(2,128)} %bitcast.8), kind=kLoop, calls=%fused_computation.113 | loop fusion | bytes 8388608 | tf_op jit(solution)/shard_map/slice | solution.py:115
  127.4 4.5 copy.49
  131.9 6.0 %copy.50 = f32[1,8,256,256]{3,2,1,0:T(8,128)} copy(f32[1,8,256,256]{2,0,3,1:T(1,128)} %get-tuple-element.304) | data formatting | bytes 4194304 | tf_op jit(solution)/shard_map/slice | solution.py:115
  138.0 240.8 %while.19 = (s32[]{:T(128)}, f32[2048,256]{1,0:T(8,128)}, f32[2048,256]{1,0:T(8,128)}, f32[8,256]{1,0:T(8,128)S(1)}, f32[8,256]{1,0:T(8,128)S(1)}, /*index=5*/f3...) while((s32[]{:T(128)}, f32[2048,256]{1,0:T(8,128)}, ...), condition=%wide.region_2.3_spmd.clone.clone, body=%wide.region_0.2_spmd.clone.clone.sunk | while | flops 1617155328 | bytes 74435056 | solution.py:79
  143.8 3.5 fusion.80
  151.2 3.3 multiply_add_fusion.22
  155.4 4.0 fusion.89
  159.4 2.6 copy.106
  162.0 4.9 fusion.90
  172.8 3.5 fusion.80
  180.3 3.3 multiply_add_fusion.22
  184.4 4.0 fusion.89
  188.4 2.6 copy.106
  191.0 6.2 %fusion.90 = (f32[2048,256]{1,0:T(8,128)}, f32[2048,256]{1,0:T(8,128)}) fusion(f32[16,128,256]{2,1,0:T(8,128)} %copy.106, f32[2048,256]{1,0:T(8,128)} %get-tuple-element.414, f32[256]{0:T(256)S(1)} %bitcast.142, pred[]{:T(512)S(6)} %compare.24, f32[16,128,256]{2,1,0:T(8,128)} %multiply_add_fusion.22, f32[2048,256]{1,0:T(8,128)} %get-tuple-element.413), kind=kLoop, calls=%fused_computation.3.clone.1 | loop fusion | flops 3145728 | bytes 12583937 | tf_op jit(solution)/shard_map/while/body/eval_jaxpr/add | solution.py:69
  203.0 3.5 fusion.80
  210.5 3.3 multiply_add_fusion.22
  214.6 4.0 fusion.89
  218.7 2.6 copy.106
  221.3 6.2 %fusion.90 = (f32[2048,256]{1,0:T(8,128)}, f32[2048,256]{1,0:T(8,128)}) fusion(f32[16,128,256]{2,1,0:T(8,128)} %copy.106, f32[2048,256]{1,0:T(8,128)} %get-tuple-element.414, f32[256]{0:T(256)S(1)} %bitcast.142, pred[]{:T(512)S(6)} %compare.24, f32[16,128,256]{2,1,0:T(8,128)} %multiply_add_fusion.22, f32[2048,256]{1,0:T(8,128)} %get-tuple-element.413), kind=kLoop, calls=%fused_computation.3.clone.1 | loop fusion | flops 3145728 | bytes 12583937 | tf_op jit(solution)/shard_map/while/body/eval_jaxpr/add | solution.py:69
  233.3 3.5 fusion.80
  240.8 3.3 multiply_add_fusion.22
  244.9 4.0 fusion.89
  248.9 2.6 copy.106
  251.5 6.2 %fusion.90 = (f32[2048,256]{1,0:T(8,128)}, f32[2048,256]{1,0:T(8,128)}) fusion(f32[16,128,256]{2,1,0:T(8,128)} %copy.106, f32[2048,256]{1,0:T(8,128)} %get-tuple-element.414, f32[256]{0:T(256)S(1)} %bitcast.142, pred[]{:T(512)S(6)} %compare.24, f32[16,128,256]{2,1,0:T(8,128)} %multiply_add_fusion.22, f32[2048,256]{1,0:T(8,128)} %get-tuple-element.413), kind=kLoop, calls=%fused_computation.3.clone.1 | loop fusion | flops 3145728 | bytes 12583937 | tf_op jit(solution)/shard_map/while/body/eval_jaxpr/add | solution.py:69
  263.6 3.5 fusion.80
  271.0 3.3 multiply_add_fusion.22
  275.2 4.0 fusion.89
  279.2 2.6 copy.106
  281.8 6.2 %fusion.90 = (f32[2048,256]{1,0:T(8,128)}, f32[2048,256]{1,0:T(8,128)}) fusion(f32[16,128,256]{2,1,0:T(8,128)} %copy.106, f32[2048,256]{1,0:T(8,128)} %get-tuple-element.414, f32[256]{0:T(256)S(1)} %bitcast.142, pred[]{:T(512)S(6)} %compare.24, f32[16,128,256]{2,1,0:T(8,128)} %multiply_add_fusion.22, f32[2048,256]{1,0:T(8,128)} %get-tuple-element.413), kind=kLoop, calls=%fused_computation.3.clone.1 | loop fusion | flops 3145728 | bytes 12583937 | tf_op jit(solution)/shard_map/while/body/eval_jaxpr/add | solution.py:69
  293.8 3.5 fusion.80
  301.3 3.3 multiply_add_fusion.22
  305.4 4.0 fusion.89
  309.4 2.6 copy.106
  312.0 6.2 %fusion.90 = (f32[2048,256]{1,0:T(8,128)}, f32[2048,256]{1,0:T(8,128)}) fusion(f32[16,128,256]{2,1,0:T(8,128)} %copy.106, f32[2048,256]{1,0:T(8,128)} %get-tuple-element.414, f32[256]{0:T(256)S(1)} %bitcast.142, pred[]{:T(512)S(6)} %compare.24, f32[16,128,256]{2,1,0:T(8,128)} %multiply_add_fusion.22, f32[2048,256]{1,0:T(8,128)} %get-tuple-element.413), kind=kLoop, calls=%fused_computation.3.clone.1 | loop fusion | flops 3145728 | bytes 12583937 | tf_op jit(solution)/shard_map/while/body/eval_jaxpr/add | solution.py:69
  324.1 3.5 fusion.80
  331.5 3.3 multiply_add_fusion.22
  335.7 4.0 fusion.89
  339.7 2.6 copy.106
  342.3 6.2 %fusion.90 = (f32[2048,256]{1,0:T(8,128)}, f32[2048,256]{1,0:T(8,128)}) fusion(f32[16,128,256]{2,1,0:T(8,128)} %copy.106, f32[2048,256]{1,0:T(8,128)} %get-tuple-element.414, f32[256]{0:T(256)S(1)} %bitcast.142, pred[]{:T(512)S(6)} %compare.24, f32[16,128,256]{2,1,0:T(8,128)} %multiply_add_fusion.22, f32[2048,256]{1,0:T(8,128)} %get-tuple-element.413), kind=kLoop, calls=%fused_computation.3.clone.1 | loop fusion | flops 3145728 | bytes 12583937 | tf_op jit(solution)/shard_map/while/body/eval_jaxpr/add | solution.py:69
  354.3 3.5 fusion.80
  361.8 3.3 multiply_add_fusion.22
  365.9 4.0 fusion.89
  369.9 2.6 copy.106
  372.6 6.2 %fusion.90 = (f32[2048,256]{1,0:T(8,128)}, f32[2048,256]{1,0:T(8,128)}) fusion(f32[16,128,256]{2,1,0:T(8,128)} %copy.106, f32[2048,256]{1,0:T(8,128)} %get-tuple-element.414, f32[256]{0:T(256)S(1)} %bitcast.142, pred[]{:T(512)S(6)} %compare.24, f32[16,128,256]{2,1,0:T(8,128)} %multiply_add_fusion.22, f32[2048,256]{1,0:T(8,128)} %get-tuple-element.413), kind=kLoop, calls=%fused_computation.3.clone.1 | loop fusion | flops 3145728 | bytes 12583937 | tf_op jit(solution)/shard_map/while/body/eval_jaxpr/add | solution.py:69
  378.8 3.4 stack.21
  383.7 4.1 pad_maximum_fusion.7
  387.8 51.5 %all_to_all.30 = f32[2,2048,256]{2,0,1:T(2,128)S(1)} all-to-all(f32[2,2048,256]{2,0,1:T(2,128)S(1)} %pad_maximum_fusion.7), channel_id=1, replica_groups=mesh['ctx'=8,'tp'=4] {'ctx'}, dimensions={1} | all-to-all | bytes 8388608 | tf_op jit(solution)/shard_map/all_to_all | solution.py:117
  439.3 2.4 copy.97
  445.1 3.5 multiply_convert_fusion
  450.9 21.4 %fusion.46 = f32[1,128,2048]{2,0,1:T(1,128)S(1)} fusion(f32[256,1,2048]{2,0,1:T(8,128)S(1)} %bitcast.128, f32[1,383,2048]{2,1,0:T(8,128)S(1)} %copy-done.19), kind=kOutput, calls=%fused_computation.96 | convolution fusion | flops 805306368 | bytes 6283264 | tf_op jit(solution)/shard_map/conv_general_dilated | solution.py:19
  472.7 5.2 rev.16
  477.9 9.9 %all_gather.3 = f32[8,2048]{1,0:T(8,128)S(1)} all-gather(f32[8,256]{1,0:T(8,128)S(1)} %get-tuple-element.201), channel_id=1, replica_groups=mesh['ctx'=8,'tp'=4] {'ctx'}, dimensions={1}, use_global_device_ids=true | all-gather | bytes 73728 | tf_op jit(solution)/shard_map/all_gather | solution.py:122
  488.4 47.4 %all-reduce.20.cloned.1.call-done = f32[128,2048]{1,0:T(8,128)} async-done(((f32[128,2048]{1,0:T(8,128)}), f32[128,2048]{1,0:T(8,128)}) %all-reduce.20.cloned.1.call-update) | async-done | bytes 1048592 | tf_op jit(solution)/shard_map/psum | solution.py:133
  535.8 2.3 broadcast_multiply_fusion
  539.7 21.8 %fusion.38 = f32[1,256,2048]{2,0,1:T(1,128)S(1)} fusion(f32[1,383,2048]{2,1,0:T(8,128)S(1)} %maximum_bitcast_fusion, f32[128,1,2048]{2,0,1:T(8,128)S(1)} %bitcast.139), kind=kOutput, calls=%fused_computation.81 | convolution fusion | flops 805306368 | bytes 6283264 | tf_op jit(solution)/shard_map/conv_general_dilated | solution.py:19
  561.5 2.5 fusion.44
  (718 shorter events, 90.4 us)
Async XLA Ops:
  7.2 61.6 %copy-start = (f32[8,2048]{1,0:T(8,128)S(1)}, f32[8,2048]{1,0:T(8,128)}, u32[]{:S(2)}) copy-start(f32[8,2048]{1,0:T(8,128)} %param.19) | copy-start | bytes 196612
  7.2 20.7 %copy-start.9 = (bf16[256,2048]{1,0:T(8,128)(2,1)S(1)}, bf16[256,2048]{1,0:T(8,128)(2,1)}, u32[]{:S(2)}) copy-start(bf16[256,2048]{1,0:T(8,128)(2,1)} %param.12) | copy-start | bytes 3145732
  7.2 20.7 %copy-start.11 = (bf16[256,2048]{1,0:T(8,128)(2,1)S(1)}, bf16[256,2048]{1,0:T(8,128)(2,1)}, u32[]{:S(2)}) copy-start(bf16[256,2048]{1,0:T(8,128)(2,1)} %param.13) | copy-start | bytes 3145732
  9.3 18.5 %collective-permute-start = (bf16[127,2048]{1,0:T(8,128)(2,1)}, bf16[127,2048]{1,0:T(8,128)(2,1)S(1)}, u32[]{:S(2)}, u32[]{:S(2)}) collective-permute-start(bf16[127,2048]{1,0:T(8,128)(2,1)} %slice.393), channel_id=1, source_target_pairs={{0,4},{4,8},{8,12},{12,16},{16,20},{20,24},{24,28},{1,5},{5,9},{9,... | collective-permute-start | bytes 1560584 | tf_op jit(solution)/shard_map/ppermute | solution.py:14
  13.7 14.1 %collective-permute-start.1 = (bf16[127,2048]{1,0:T(8,128)(2,1)}, bf16[127,2048]{1,0:T(8,128)(2,1)}, u32[]{:S(2)}, u32[]{:S(2)}) collective-permute-start(bf16[127,2048]{1,0:T(8,128)(2,1)} %slice.394), channel_id=1, source_target_pairs={{0,4},{4,8},{8,12},{12,16},{16,20},{20,24},{24,28},{1,5},{5,9},{9,... | collective-permute-start | bytes 1560584 | tf_op jit(solution)/shard_map/ppermute | solution.py:14
  27.9 3.4 copy-start.22
  29.6 1.6 copy-start.18
  31.3 21.6 %copy-start.13 = (bf16[256,2048]{1,0:T(8,128)(2,1)S(1)}, bf16[256,2048]{1,0:T(8,128)(2,1)}, u32[]{:S(2)}) copy-start(bf16[256,2048]{1,0:T(8,128)(2,1)} %param.15) | copy-start | bytes 3145732
  31.3 21.6 %copy-start.14 = (bf16[256,2048]{1,0:T(8,128)(2,1)S(1)}, bf16[256,2048]{1,0:T(8,128)(2,1)}, u32[]{:S(2)}) copy-start(bf16[256,2048]{1,0:T(8,128)(2,1)} %param.11) | copy-start | bytes 3145732
  31.3 21.6 %copy-start.16 = (bf16[256,2048]{1,0:T(8,128)(2,1)S(1)}, bf16[256,2048]{1,0:T(8,128)(2,1)}, u32[]{:S(2)}) copy-start(bf16[256,2048]{1,0:T(8,128)(2,1)} %param.16) | copy-start | bytes 3145732
  31.3 21.6 %copy-start.20 = (bf16[256,2048]{1,0:T(8,128)(2,1)S(1)}, bf16[256,2048]{1,0:T(8,128)(2,1)}, u32[]{:S(2)}) copy-start(bf16[256,2048]{1,0:T(8,128)(2,1)} %param.14) | copy-start | bytes 3145732
  52.9 1.5 copy-start.7
  64.1 53.7 %all-to-all-start = ((f32[2,256,2048]{1,0,2:T(2,128)}), f32[2,256,2048]{1,0,2:T(2,128)}, u32[]{:S(2)}, u32[]{:S(2)}) async-start(f32[2,256,2048]{1,0,2:T(2,128)} %copy.48), calls=%async_computation | async-start | bytes 8388608 | tf_op jit(solution)/shard_map/all_to_all | solution.py:107
  68.7 467.2 %all-reduce.20.cloned.1.call-start = ((), (), s32[]{:S(2)}) async-start(), calls=%async_computation.2 | async-start | bytes 2097152 | tf_op jit(solution)/shard_map/psum | solution.py:133
  131.9 6.1 %copy-start.23 = (f32[8]{0:T(128)S(1)}, f32[8]{0:T(128)}, u32[]{:S(2)}) copy-start(f32[8]{0:T(128)} %param.18) | copy-start | bytes 100
  138.0 4.1 copy-start.2
  142.1 1.3 copy-start.4
  148.5 1.4 copy-start.6
  162.0 5.0 copy-start.3
  167.0 4.1 copy-start.2
  171.1 1.3 copy-start.4
  177.5 1.4 copy-start.6
  191.0 6.2 %copy-start.3 = (f32[2048,256]{1,0:T(8,128)S(1)}, f32[2048,256]{1,0:T(8,128)}, u32[]{:S(2)}) copy-start(f32[2048,256]{1,0:T(8,128)} %copy-done.2) | copy-start | bytes 6291460 | tf_op jit(solution)/shard_map/while
  197.2 4.1 copy-start.2
  201.3 1.3 copy-start.4
  207.8 1.4 copy-start.6
  221.3 6.2 %copy-start.3 = (f32[2048,256]{1,0:T(8,128)S(1)}, f32[2048,256]{1,0:T(8,128)}, u32[]{:S(2)}) copy-start(f32[2048,256]{1,0:T(8,128)} %copy-done.2) | copy-start | bytes 6291460 | tf_op jit(solution)/shard_map/while
  227.5 4.1 copy-start.2
  231.6 1.3 copy-start.4
  238.0 1.4 copy-start.6
  251.5 6.2 %copy-start.3 = (f32[2048,256]{1,0:T(8,128)S(1)}, f32[2048,256]{1,0:T(8,128)}, u32[]{:S(2)}) copy-start(f32[2048,256]{1,0:T(8,128)} %copy-done.2) | copy-start | bytes 6291460 | tf_op jit(solution)/shard_map/while
  257.8 4.1 copy-start.2
  261.8 1.3 copy-start.4
  268.3 1.4 copy-start.6
  281.8 6.2 %copy-start.3 = (f32[2048,256]{1,0:T(8,128)S(1)}, f32[2048,256]{1,0:T(8,128)}, u32[]{:S(2)}) copy-start(f32[2048,256]{1,0:T(8,128)} %copy-done.2) | copy-start | bytes 6291460 | tf_op jit(solution)/shard_map/while
  288.0 4.1 copy-start.2
  292.1 1.3 copy-start.4
  298.5 1.4 copy-start.6
  312.0 6.2 %copy-start.3 = (f32[2048,256]{1,0:T(8,128)S(1)}, f32[2048,256]{1,0:T(8,128)}, u32[]{:S(2)}) copy-start(f32[2048,256]{1,0:T(8,128)} %copy-done.2) | copy-start | bytes 6291460 | tf_op jit(solution)/shard_map/while
  318.3 4.1 copy-start.2
  322.4 1.3 copy-start.4
  328.8 1.4 copy-start.6
  342.3 6.2 %copy-start.3 = (f32[2048,256]{1,0:T(8,128)S(1)}, f32[2048,256]{1,0:T(8,128)}, u32[]{:S(2)}) copy-start(f32[2048,256]{1,0:T(8,128)} %copy-done.2) | copy-start | bytes 6291460 | tf_op jit(solution)/shard_map/while
  348.5 4.1 copy-start.2
  352.6 1.3 copy-start.4
  359.0 1.4 copy-start.6
  372.6 6.2 %copy-start.3 = (f32[2048,256]{1,0:T(8,128)S(1)}, f32[2048,256]{1,0:T(8,128)}, u32[]{:S(2)}) copy-start(f32[2048,256]{1,0:T(8,128)} %copy-done.2) | copy-start | bytes 6291460 | tf_op jit(solution)/shard_map/while
  378.8 3.4 copy-start.5
  442.9 1.6 copy-start.8
  442.9 1.8 copy-start.15
  443.0 2.1 copy-start.17
  445.1 5.8 %copy-start.19 = (f32[1,383,2048]{2,1,0:T(8,128)S(1)}, f32[1,383,2048]{2,1,0:T(8,128)}, u32[]{:S(2)}) copy-start(f32[1,383,2048]{2,1,0:T(8,128)} %copy-done.18) | copy-start | bytes 9412612
  449.6 88.5 %collective-permute-start.2 = (f32[127,2048]{1,0:T(8,128)}, f32[127,2048]{1,0:T(8,128)}, u32[]{:S(2)}, u32[]{:S(2)}) collective-permute-start(f32[127,2048]{1,0:T(8,128)} %slice.517), channel_id=1, source_target_pairs={{4,0},{8,4},{12,8},{16,12},{20,16},{24,20},{28,24},{5,1},{9,5},{13... | collective-permute-start | bytes 3121160 | tf_op jit(solution)/shard_map/ppermute | solution.py:14
  538.1 1.5 copy-start.21
  539.7 21.8 %copy-start.10 = (bf16[256,2048]{1,0:T(8,128)(2,1)S(1)}, bf16[256,2048]{1,0:T(8,128)(2,1)}, u32[]{:S(2)}) copy-start(bf16[256,2048]{1,0:T(8,128)(2,1)} %param.12) | copy-start | bytes 3145732
  539.7 21.8 %copy-start.12 = (bf16[256,2048]{1,0:T(8,128)(2,1)S(1)}, bf16[256,2048]{1,0:T(8,128)(2,1)}, u32[]{:S(2)}) copy-start(bf16[256,2048]{1,0:T(8,128)(2,1)} %param.13) | copy-start | bytes 3145732
  539.7 24.3 %copy-start.1 = (f32[8,2048]{1,0:T(8,128)S(1)}, f32[8,2048]{1,0:T(8,128)}, u32[]{:S(2)}) copy-start(f32[8,2048]{1,0:T(8,128)} %param.19) | copy-start | bytes 196612
Sparse Core Ops, SparseCore 0:
  478.0 57.7 all-reduce.19
where the time goes:
time: 574 us; the launch traced here: 571 us
  local copies, waits for them, and re-layouts  134 us (23%)
  other arithmetic  128 us (22%)
  matrix products  108 us (19%)
  waiting for transfers between devices  96.4 us (17%)
  blocking collectives  61.4 us (11%)
  between operations  14.4 us (3%)
  loops' own time  13.9 us (2%)
  starting transfers between devices  13.6 us (2%)
    conv_general_dilated x3, matrix products, depthwise(): lax.conv_general_dilated(signal[None], kernel[:, None, :], (1,), 'VALID',...  64.7 us
    all_to_all x1, blocking collectives, per_device(): lax.all_to_all(jnp.stack([conv_seq, back_seq]), 'ctx', split_axis=1, conc...  51.5 us
    all_to_all x1, waiting for transfers between devices, per_device(): lax.all_to_all(jnp.stack([li_input, li_cotan]), 'ctx', split_axis=2, conc...  49 us
    add x8, other arithmetic, one_mode(): back_sum = back_sum + residue_row[None, :] * reverse_states  48.2 us
    psum x1, waiting for transfers between devices, per_device(): tap_sum = lax.psum(tap_part, 'ctx')  47.4 us
    reduce_sum x8, other arithmetic, one_mode(): jnp.sum(inputs * reverse_states, 0)  32.1 us
    dot_general x8, matrix products, one_mode(): backward = jnp.einsum('jt,bjc->btc', toeplitz, co_blocks, precision=highest)  27.8 us
    add x8, other arithmetic, one_mode(): forward + lead_pows[None, :, None] * forward_in[:, None, :]  26.2 us
  transfers between devices with their start and end apart: 5, of which 2 were waited for; matrix products, arithmetic and copies ran while one was open for 7% of the time, Pallas kernels for 0%

commit v1 on v0

--- a/solution.py
+++ b/solution.py
@@ -130,7 +130,7 @@
     grad_key_mr = (mixed_grad * value_first).astype(jnp.bfloat16)
     grad_value_mr = (mixed_grad * key_first).astype(jnp.bfloat16)
     tap_part = depthwise(mixed_in, mr_cotan)[::-1]
-    tap_sum = lax.psum(tap_part, "ctx")
+    tap_sum = jnp.sum(lax.all_gather(tap_part, "ctx"), axis=0)
     factor = 1.0 / math.sqrt(seq_len)
     return (
         grad_query_mr,

time: 574 us -> 551 us (0.960)
  waiting for transfers between devices: 96.4 us -> 54.2 us
  blocking collectives: 61.4 us -> 79.5 us
    psum x1 -> x0, waiting for transfers between devices: 47.4 us -> none  [per_device(): tap_sum = lax.psum(tap_part, 'ctx')]
    all_gather x1, blocking collectives: 9.89 us -> 27.9 us  [per_device(): residue_sum = lax.all_gather(residue_piece, 'ctx', axis=1, tiled=True)]
where the time goes in v1:
time: 551 us; the launch traced here: 548 us
  local copies, waits for them, and re-layouts  134 us (24%)
  other arithmetic  130 us (24%)
  matrix products  108 us (20%)
  blocking collectives  79.5 us (14%)
  waiting for transfers between devices  54.2 us (10%)
  between operations  14.4 us (3%)
  loops' own time  13.9 us (3%)
  starting transfers between devices  13.6 us (2%)
    conv_general_dilated x3, matrix products, depthwise(): lax.conv_general_dilated(signal[None], kernel[:, None, :], (1,), 'VALID',...  64.3 us
    all_to_all x1, blocking collectives, per_device(): lax.all_to_all(jnp.stack([conv_seq, back_seq]), 'ctx', split_axis=1, conc...  51.5 us
    all_to_all x1, waiting for transfers between devices, per_device(): lax.all_to_all(jnp.stack([li_input, li_cotan]), 'ctx', split_axis=2, conc...  49 us
    add x8, other arithmetic, one_mode(): back_sum = back_sum + residue_row[None, :] * reverse_states  48.2 us
    reduce_sum x8, other arithmetic, one_mode(): jnp.sum(inputs * reverse_states, 0)  32.1 us
    all_gather x1, blocking collectives, per_device(): residue_sum = lax.all_gather(residue_piece, 'ctx', axis=1, tiled=True)  27.9 us
    dot_general x8, matrix products, one_mode(): backward = jnp.einsum('jt,bjc->btc', toeplitz, co_blocks, precision=highest)  27.8 us
    add x8, other arithmetic, one_mode(): forward + lead_pows[None, :, None] * forward_in[:, None, :]  26.2 us
  transfers between devices with their start and end apart: 5, of which 2 were waited for; matrix products, arithmetic and copies ran while one was open for 7% of the time, Pallas kernels for 0%

profile of v1, /device:TPU:0, one launch (start us, length us, event | category | flops | bytes accessed | tf_op | source)
XLA Modules:
  0.0 547.8 jit_solution(1416313584409371274)
XLA Ops:
  9.3 2.4 collective-permute-start
  13.7 5.3 collective-permute-start.1
  19.0 8.9 %rev.15 = f32[128,2048]{1,0:T(8,128)} reverse(f32[128,2048]{1,0:T(8,128)} %param.17), dimensions={0} | reverse | bytes 2097152 | tf_op jit(solution)/shard_map/rev | solution.py:101
  31.3 21.5 %fusion.49 = f32[1,256,2048]{2,0,1:T(1,128)S(1)} fusion(f32[1,383,2048]{2,1,0:T(8,128)S(1)} %convert_multiply_fusion, f32[128,1,2048]{2,0,1:T(8,128)S(1)} %bitcast.142), kind=kOutput, calls=%fused_computation.100 | convolution fusion | flops 805306368 | bytes 6283264 | tf_op jit(solution)/shard_map/conv_general_dilated | solution.py:19
  54.4 2.5 pad_maximum_fusion.6
  56.9 7.3 %copy.48 = f32[2,256,2048]{1,0,2:T(2,128)} copy(f32[2,256,2048]{2,1,0:T(8,128)} %pad_maximum_fusion.6) | data formatting | bytes 8388608 | tf_op jit(solution)/shard_map/stack | solution.py:108
  64.1 4.6 all-to-all-start
  68.8 49.0 %all-to-all-done = f32[2,256,2048]{1,0,2:T(2,128)} async-done(((f32[2,256,2048]{1,0,2:T(2,128)}), f32[2,256,2048]{1,0,2:T(2,128)}, u32[]{:S(2)}, u32[]{:S(2)}) %all-to-all-start) | async-done | bytes 4194336 | tf_op jit(solution)/shard_map/all_to_all | solution.py:107
  117.8 9.6 %fusion.58 = (f32[1,8,256,256]{2,0,3,1:T(1,128)}, f32[1,8,256,256]{2,0,3,1:T(1,128)}) fusion(f32[2,8,256,256]{2,0,3,1:T(2,128)} %bitcast.8), kind=kLoop, calls=%fused_computation.113 | loop fusion | bytes 8388608 | tf_op jit(solution)/shard_map/slice | solution.py:115
  127.4 4.5 copy.49
  131.9 6.0 %copy.50 = f32[1,8,256,256]{3,2,1,0:T(8,128)} copy(f32[1,8,256,256]{2,0,3,1:T(1,128)} %get-tuple-element.304) | data formatting | bytes 4194304 | tf_op jit(solution)/shard_map/slice | solution.py:115
  138.0 240.8 %while.19 = (s32[]{:T(128)}, f32[2048,256]{1,0:T(8,128)}, f32[2048,256]{1,0:T(8,128)}, f32[8,256]{1,0:T(8,128)S(1)}, f32[8,256]{1,0:T(8,128)S(1)}, /*index=5*/f3...) while((s32[]{:T(128)}, f32[2048,256]{1,0:T(8,128)}, ...), condition=%wide.region_2.3_spmd.clone.clone, body=%wide.region_0.2_spmd.clone.clone.sunk | while | flops 1617155328 | bytes 74435056 | solution.py:79
  143.8 3.5 fusion.80
  151.2 3.3 multiply_add_fusion.22
  155.4 4.0 fusion.89
  159.4 2.6 copy.106
  162.0 4.9 fusion.90
  172.8 3.5 fusion.80
  180.3 3.3 multiply_add_fusion.22
  184.4 4.0 fusion.89
  188.4 2.6 copy.106
  191.0 6.2 %fusion.90 = (f32[2048,256]{1,0:T(8,128)}, f32[2048,256]{1,0:T(8,128)}) fusion(f32[16,128,256]{2,1,0:T(8,128)} %copy.106, f32[2048,256]{1,0:T(8,128)} %get-tuple-element.414, f32[256]{0:T(256)S(1)} %bitcast.144, pred[]{:T(512)S(6)} %compare.24, f32[16,128,256]{2,1,0:T(8,128)} %multiply_add_fusion.22, f32[2048,256]{1,0:T(8,128)} %get-tuple-element.413), kind=kLoop, calls=%fused_computation.3.clone.1 | loop fusion | flops 3145728 | bytes 12583937 | tf_op jit(solution)/shard_map/while/body/eval_jaxpr/add | solution.py:69
  203.0 3.5 fusion.80
  210.5 3.3 multiply_add_fusion.22
  214.6 4.0 fusion.89
  218.7 2.6 copy.106
  221.3 6.2 %fusion.90 = (f32[2048,256]{1,0:T(8,128)}, f32[2048,256]{1,0:T(8,128)}) fusion(f32[16,128,256]{2,1,0:T(8,128)} %copy.106, f32[2048,256]{1,0:T(8,128)} %get-tuple-element.414, f32[256]{0:T(256)S(1)} %bitcast.144, pred[]{:T(512)S(6)} %compare.24, f32[16,128,256]{2,1,0:T(8,128)} %multiply_add_fusion.22, f32[2048,256]{1,0:T(8,128)} %get-tuple-element.413), kind=kLoop, calls=%fused_computation.3.clone.1 | loop fusion | flops 3145728 | bytes 12583937 | tf_op jit(solution)/shard_map/while/body/eval_jaxpr/add | solution.py:69
  233.3 3.5 fusion.80
  240.8 3.3 multiply_add_fusion.22
  244.9 4.0 fusion.89
  248.9 2.6 copy.106
  251.5 6.2 %fusion.90 = (f32[2048,256]{1,0:T(8,128)}, f32[2048,256]{1,0:T(8,128)}) fusion(f32[16,128,256]{2,1,0:T(8,128)} %copy.106, f32[2048,256]{1,0:T(8,128)} %get-tuple-element.414, f32[256]{0:T(256)S(1)} %bitcast.144, pred[]{:T(512)S(6)} %compare.24, f32[16,128,256]{2,1,0:T(8,128)} %multiply_add_fusion.22, f32[2048,256]{1,0:T(8,128)} %get-tuple-element.413), kind=kLoop, calls=%fused_computation.3.clone.1 | loop fusion | flops 3145728 | bytes 12583937 | tf_op jit(solution)/shard_map/while/body/eval_jaxpr/add | solution.py:69
  263.6 3.5 fusion.80
  271.0 3.3 multiply_add_fusion.22
  275.2 4.0 fusion.89
  279.2 2.6 copy.106
  281.8 6.2 %fusion.90 = (f32[2048,256]{1,0:T(8,128)}, f32[2048,256]{1,0:T(8,128)}) fusion(f32[16,128,256]{2,1,0:T(8,128)} %copy.106, f32[2048,256]{1,0:T(8,128)} %get-tuple-element.414, f32[256]{0:T(256)S(1)} %bitcast.144, pred[]{:T(512)S(6)} %compare.24, f32[16,128,256]{2,1,0:T(8,128)} %multiply_add_fusion.22, f32[2048,256]{1,0:T(8,128)} %get-tuple-element.413), kind=kLoop, calls=%fused_computation.3.clone.1 | loop fusion | flops 3145728 | bytes 12583937 | tf_op jit(solution)/shard_map/while/body/eval_jaxpr/add | solution.py:69
  293.8 3.5 fusion.80
  301.3 3.3 multiply_add_fusion.22
  305.4 4.0 fusion.89
  309.4 2.6 copy.106
  312.0 6.2 %fusion.90 = (f32[2048,256]{1,0:T(8,128)}, f32[2048,256]{1,0:T(8,128)}) fusion(f32[16,128,256]{2,1,0:T(8,128)} %copy.106, f32[2048,256]{1,0:T(8,128)} %get-tuple-element.414, f32[256]{0:T(256)S(1)} %bitcast.144, pred[]{:T(512)S(6)} %compare.24, f32[16,128,256]{2,1,0:T(8,128)} %multiply_add_fusion.22, f32[2048,256]{1,0:T(8,128)} %get-tuple-element.413), kind=kLoop, calls=%fused_computation.3.clone.1 | loop fusion | flops 3145728 | bytes 12583937 | tf_op jit(solution)/shard_map/while/body/eval_jaxpr/add | solution.py:69
  324.1 3.5 fusion.80
  331.5 3.3 multiply_add_fusion.22
  335.7 4.0 fusion.89
  339.7 2.6 copy.106
  342.3 6.2 %fusion.90 = (f32[2048,256]{1,0:T(8,128)}, f32[2048,256]{1,0:T(8,128)}) fusion(f32[16,128,256]{2,1,0:T(8,128)} %copy.106, f32[2048,256]{1,0:T(8,128)} %get-tuple-element.414, f32[256]{0:T(256)S(1)} %bitcast.144, pred[]{:T(512)S(6)} %compare.24, f32[16,128,256]{2,1,0:T(8,128)} %multiply_add_fusion.22, f32[2048,256]{1,0:T(8,128)} %get-tuple-element.413), kind=kLoop, calls=%fused_computation.3.clone.1 | loop fusion | flops 3145728 | bytes 12583937 | tf_op jit(solution)/shard_map/while/body/eval_jaxpr/add | solution.py:69
  354.3 3.5 fusion.80
  361.8 3.3 multiply_add_fusion.22
  365.9 4.0 fusion.89
  369.9 2.6 copy.106
  372.6 6.2 %fusion.90 = (f32[2048,256]{1,0:T(8,128)}, f32[2048,256]{1,0:T(8,128)}) fusion(f32[16,128,256]{2,1,0:T(8,128)} %copy.106, f32[2048,256]{1,0:T(8,128)} %get-tuple-element.414, f32[256]{0:T(256)S(1)} %bitcast.144, pred[]{:T(512)S(6)} %compare.24, f32[16,128,256]{2,1,0:T(8,128)} %multiply_add_fusion.22, f32[2048,256]{1,0:T(8,128)} %get-tuple-element.413), kind=kLoop, calls=%fused_computation.3.clone.1 | loop fusion | flops 3145728 | bytes 12583937 | tf_op jit(solution)/shard_map/while/body/eval_jaxpr/add | solution.py:69
  378.8 3.4 stack.21
  383.7 4.1 pad_maximum_fusion.7
  387.8 51.5 %all_to_all.30 = f32[2,2048,256]{2,0,1:T(2,128)S(1)} all-to-all(f32[2,2048,256]{2,0,1:T(2,128)S(1)} %pad_maximum_fusion.7), channel_id=1, replica_groups=mesh['ctx'=8,'tp'=4] {'ctx'}, dimensions={1} | all-to-all | bytes 8388608 | tf_op jit(solution)/shard_map/all_to_all | solution.py:117
  439.3 2.4 copy.97
  445.1 3.5 multiply_convert_fusion
  448.6 21.3 %fusion.46 = f32[1,128,2048]{2,0,1:T(1,128)S(1)} fusion(f32[256,1,2048]{2,0,1:T(8,128)S(1)} %bitcast.129, f32[1,383,2048]{2,1,0:T(8,128)S(1)} %copy-done.19), kind=kOutput, calls=%fused_computation.96 | convolution fusion | flops 805306368 | bytes 6283264 | tf_op jit(solution)/shard_map/conv_general_dilated | solution.py:19
  470.3 5.2 rev.16
  476.9 27.9 %all_gather.11 = f32[8,2048]{1,0:T(8,128)S(1)} all-gather(f32[8,256]{1,0:T(8,128)S(1)} %get-tuple-element.201), channel_id=1, replica_groups=mesh['ctx'=8,'tp'=4] {'ctx'}, dimensions={1}, use_global_device_ids=true | all-gather | bytes 73728 | tf_op jit(solution)/shard_map/all_gather | solution.py:122
  506.7 21.5 %fusion.38 = f32[1,256,2048]{2,0,1:T(1,128)S(1)} fusion(f32[1,383,2048]{2,1,0:T(8,128)S(1)} %maximum_bitcast_fusion, f32[128,1,2048]{2,0,1:T(8,128)S(1)} %bitcast.141), kind=kOutput, calls=%fused_computation.81 | convolution fusion | flops 805306368 | bytes 6283264 | tf_op jit(solution)/shard_map/conv_general_dilated | solution.py:19
  528.2 2.4 fusion.44
  530.6 5.2 all-gather.3.cloned.1.call-done
  535.7 4.2 reduce_sum.22
  (719 shorter events, 90.2 us)
Async XLA Ops:
  7.2 61.6 %copy-start = (f32[8,2048]{1,0:T(8,128)S(1)}, f32[8,2048]{1,0:T(8,128)}, u32[]{:S(2)}) copy-start(f32[8,2048]{1,0:T(8,128)} %param.19) | copy-start | bytes 196612
  7.2 20.7 %copy-start.9 = (bf16[256,2048]{1,0:T(8,128)(2,1)S(1)}, bf16[256,2048]{1,0:T(8,128)(2,1)}, u32[]{:S(2)}) copy-start(bf16[256,2048]{1,0:T(8,128)(2,1)} %param.12) | copy-start | bytes 3145732
  7.2 20.7 %copy-start.11 = (bf16[256,2048]{1,0:T(8,128)(2,1)S(1)}, bf16[256,2048]{1,0:T(8,128)(2,1)}, u32[]{:S(2)}) copy-start(bf16[256,2048]{1,0:T(8,128)(2,1)} %param.13) | copy-start | bytes 3145732
  9.3 18.5 %collective-permute-start = (bf16[127,2048]{1,0:T(8,128)(2,1)}, bf16[127,2048]{1,0:T(8,128)(2,1)S(1)}, u32[]{:S(2)}, u32[]{:S(2)}) collective-permute-start(bf16[127,2048]{1,0:T(8,128)(2,1)} %slice.393), channel_id=1, source_target_pairs={{0,4},{4,8},{8,12},{12,16},{16,20},{20,24},{24,28},{1,5},{5,9},{9,... | collective-permute-start | bytes 1560584 | tf_op jit(solution)/shard_map/ppermute | solution.py:14
  13.7 14.1 %collective-permute-start.1 = (bf16[127,2048]{1,0:T(8,128)(2,1)}, bf16[127,2048]{1,0:T(8,128)(2,1)}, u32[]{:S(2)}, u32[]{:S(2)}) collective-permute-start(bf16[127,2048]{1,0:T(8,128)(2,1)} %slice.394), channel_id=1, source_target_pairs={{0,4},{4,8},{8,12},{12,16},{16,20},{20,24},{24,28},{1,5},{5,9},{9,... | collective-permute-start | bytes 1560584 | tf_op jit(solution)/shard_map/ppermute | solution.py:14
  27.9 3.4 copy-start.22
  29.6 1.6 copy-start.18
  31.3 21.6 %copy-start.13 = (bf16[256,2048]{1,0:T(8,128)(2,1)S(1)}, bf16[256,2048]{1,0:T(8,128)(2,1)}, u32[]{:S(2)}) copy-start(bf16[256,2048]{1,0:T(8,128)(2,1)} %param.15) | copy-start | bytes 3145732
  31.3 21.6 %copy-start.14 = (bf16[256,2048]{1,0:T(8,128)(2,1)S(1)}, bf16[256,2048]{1,0:T(8,128)(2,1)}, u32[]{:S(2)}) copy-start(bf16[256,2048]{1,0:T(8,128)(2,1)} %param.11) | copy-start | bytes 3145732
  31.3 21.6 %copy-start.16 = (bf16[256,2048]{1,0:T(8,128)(2,1)S(1)}, bf16[256,2048]{1,0:T(8,128)(2,1)}, u32[]{:S(2)}) copy-start(bf16[256,2048]{1,0:T(8,128)(2,1)} %param.16) | copy-start | bytes 3145732
  31.3 21.6 %copy-start.20 = (bf16[256,2048]{1,0:T(8,128)(2,1)S(1)}, bf16[256,2048]{1,0:T(8,128)(2,1)}, u32[]{:S(2)}) copy-start(bf16[256,2048]{1,0:T(8,128)(2,1)} %param.14) | copy-start | bytes 3145732
  52.9 1.5 copy-start.7
  64.1 53.7 %all-to-all-start = ((f32[2,256,2048]{1,0,2:T(2,128)}), f32[2,256,2048]{1,0,2:T(2,128)}, u32[]{:S(2)}, u32[]{:S(2)}) async-start(f32[2,256,2048]{1,0,2:T(2,128)} %copy.48), calls=%async_computation | async-start | bytes 8388608 | tf_op jit(solution)/shard_map/all_to_all | solution.py:107
  68.7 467.1 %all-gather.3.cloned.1.call-start = ((), (), s32[]{:S(2)}) async-start(), calls=%async_computation.2 | async-start | bytes 9437184 | tf_op jit(solution)/shard_map/all_gather | solution.py:133
  131.9 6.1 %copy-start.23 = (f32[8]{0:T(128)S(1)}, f32[8]{0:T(128)}, u32[]{:S(2)}) copy-start(f32[8]{0:T(128)} %param.18) | copy-start | bytes 100
  138.0 4.1 copy-start.2
  142.1 1.3 copy-start.4
  148.5 1.4 copy-start.6
  162.0 5.0 copy-start.3
  167.0 4.1 copy-start.2
  171.1 1.3 copy-start.4
  177.5 1.4 copy-start.6
  191.0 6.2 %copy-start.3 = (f32[2048,256]{1,0:T(8,128)S(1)}, f32[2048,256]{1,0:T(8,128)}, u32[]{:S(2)}) copy-start(f32[2048,256]{1,0:T(8,128)} %copy-done.2) | copy-start | bytes 6291460 | tf_op jit(solution)/shard_map/while
  197.2 4.1 copy-start.2
  201.3 1.3 copy-start.4
  207.8 1.4 copy-start.6
  221.3 6.2 %copy-start.3 = (f32[2048,256]{1,0:T(8,128)S(1)}, f32[2048,256]{1,0:T(8,128)}, u32[]{:S(2)}) copy-start(f32[2048,256]{1,0:T(8,128)} %copy-done.2) | copy-start | bytes 6291460 | tf_op jit(solution)/shard_map/while
  227.5 4.1 copy-start.2
  231.6 1.3 copy-start.4
  238.0 1.4 copy-start.6
  251.5 6.2 %copy-start.3 = (f32[2048,256]{1,0:T(8,128)S(1)}, f32[2048,256]{1,0:T(8,128)}, u32[]{:S(2)}) copy-start(f32[2048,256]{1,0:T(8,128)} %copy-done.2) | copy-start | bytes 6291460 | tf_op jit(solution)/shard_map/while
  257.8 4.1 copy-start.2
  261.8 1.3 copy-start.4
  268.3 1.4 copy-start.6
  281.8 6.2 %copy-start.3 = (f32[2048,256]{1,0:T(8,128)S(1)}, f32[2048,256]{1,0:T(8,128)}, u32[]{:S(2)}) copy-start(f32[2048,256]{1,0:T(8,128)} %copy-done.2) | copy-start | bytes 6291460 | tf_op jit(solution)/shard_map/while
  288.0 4.1 copy-start.2
  292.1 1.3 copy-start.4
  298.5 1.4 copy-start.6
  312.0 6.2 %copy-start.3 = (f32[2048,256]{1,0:T(8,128)S(1)}, f32[2048,256]{1,0:T(8,128)}, u32[]{:S(2)}) copy-start(f32[2048,256]{1,0:T(8,128)} %copy-done.2) | copy-start | bytes 6291460 | tf_op jit(solution)/shard_map/while
  318.3 4.1 copy-start.2
  322.4 1.3 copy-start.4
  328.8 1.4 copy-start.6
  342.3 6.2 %copy-start.3 = (f32[2048,256]{1,0:T(8,128)S(1)}, f32[2048,256]{1,0:T(8,128)}, u32[]{:S(2)}) copy-start(f32[2048,256]{1,0:T(8,128)} %copy-done.2) | copy-start | bytes 6291460 | tf_op jit(solution)/shard_map/while
  348.5 4.1 copy-start.2
  352.6 1.3 copy-start.4
  359.0 1.4 copy-start.6
  372.6 6.2 %copy-start.3 = (f32[2048,256]{1,0:T(8,128)S(1)}, f32[2048,256]{1,0:T(8,128)}, u32[]{:S(2)}) copy-start(f32[2048,256]{1,0:T(8,128)} %copy-done.2) | copy-start | bytes 6291460 | tf_op jit(solution)/shard_map/while
  378.8 3.4 copy-start.5
  442.9 1.6 copy-start.8
  442.9 1.8 copy-start.15
  443.0 2.1 copy-start.17
  445.1 3.5 copy-start.19
  475.6 29.9 %collective-permute-start.2 = (f32[127,2048]{1,0:T(8,128)S(1)}, f32[127,2048]{1,0:T(8,128)S(1)}, u32[]{:S(2)}, u32[]{:S(2)}) collective-permute-start(f32[127,2048]{1,0:T(8,128)S(1)} %slice.517), channel_id=1, source_target_pairs={{4,0},{8,4},{12,8},{16,12},{20,16},{24,20},{28,24},{5,1},{9,5},{13... | collective-permute-start | bytes 3121160 | tf_op jit(solution)/shard_map/ppermute | solution.py:14
  505.4 1.2 copy-start.21
  506.7 21.5 %copy-start.10 = (bf16[256,2048]{1,0:T(8,128)(2,1)S(1)}, bf16[256,2048]{1,0:T(8,128)(2,1)}, u32[]{:S(2)}) copy-start(bf16[256,2048]{1,0:T(8,128)(2,1)} %param.12) | copy-start | bytes 3145732
  506.7 21.5 %copy-start.12 = (bf16[256,2048]{1,0:T(8,128)(2,1)S(1)}, bf16[256,2048]{1,0:T(8,128)(2,1)}, u32[]{:S(2)}) copy-start(bf16[256,2048]{1,0:T(8,128)(2,1)} %param.13) | copy-start | bytes 3145732
  535.7 5.3 copy-start.1
Sparse Core Ops, SparseCore 0:
  475.6 60.0 all-gather.2
